TPU v7x, 32 devices: a whole 2x2x4 slice. The times are simulated.
32 devices in a mesh: obs: 4 (over z), src: 8 (over y, x, core).
Axes of the slice: x: 2, y: 2, z: 4, core: 2. Of those that a mesh axis runs over, the one named last changes fastest.
Arguments:
- history: bfloat16 [3, 64, 64, 1536], P(None, ('obs', 'src')), may hold values from -6 to 6
- incident: bfloat16 [5, 64, 64, 1536], P(None, ('obs', 'src')), may hold values from -6 to 6
- proj_basis: bfloat16 [64, 64, 1536], P(('obs', 'src')), may hold values from -0.15625 to 0.15625
- expand_basis: bfloat16 [64, 64, 1536], P(('obs', 'src')), may hold values from -0.75 to 0.75
- near_inverse: bfloat16 [64, 1536, 1536], P(('obs', 'src')), may hold values from -0.15625 to 0.15625
- couplings: bfloat16 [2, 4096, 4, 8, 128], P(None, 'obs', None, 'src'), may hold values from -0.09375 to 0.09375
- lags: int32 [64, 4, 8, 2], P('obs', None, 'src'), may hold values from 0 to 2, as said below
Outputs:
- currents: bfloat16 [5, 64, 64, 1536], P(None, ('obs', 'src'))
Inputs may be any that keep to these rules, and one draw needn't show every extreme that they name: lags[j, o, s, k] is the lag from source cluster j to observer cluster (o * 8 + s) * 2 + k. Entries are 0, 1 or 2, and the entry of every cluster with itself is 0.
All inputs are finite; a program needn't handle non-finite values.
Results may differ from a plain program's by a relative error of at most 0.025.
Values may be sent and summed in bfloat16 or wider, within the bound.
A program may use at most 192 MiB of HBM per device.

v0:
```python
import jax
import jax.numpy as jnp
from jax import lax
from jax.sharding import PartitionSpec as P

STEPS = 5
TAPS = 2
HIST = 3


def per_device(history, incident, proj_basis, expand_basis, near_inverse, couplings, lags):
    rank = proj_basis.shape[1]
    local_clusters = proj_basis.shape[0]
    excite = history.shape[2]
    src_rows = couplings.shape[1]
    obs_cols = couplings.shape[2] * couplings.shape[3] * couplings.shape[4]
    src_clusters = lags.shape[0]
    obs_clusters = lags.shape[1] * lags.shape[2] * lags.shape[3]
    kernel = couplings.reshape(TAPS, src_clusters, rank, obs_clusters, rank)
    lag_pairs = lags.reshape(src_clusters, obs_clusters)
    matrices = []
    for delay in range(1, HIST + 1):
        combined = jnp.zeros_like(kernel[0])
        for tap_index in range(TAPS):
            if delay - tap_index >= 1:
                chosen = (lag_pairs == delay - tap_index)[:, None, :, None]
                combined = jnp.where(chosen, kernel[tap_index], combined)
        matrices.append(combined.reshape(src_rows, obs_cols))

    def project(current):
        projected = jnp.einsum(
            "ceb,crb->ecr", current, proj_basis, preferred_element_type=jnp.float32
        )
        return projected.astype(jnp.bfloat16).reshape(excite, local_clusters * rank)

    def couple(columns, delay):
        return jnp.dot(columns, matrices[delay - 1], preferred_element_type=jnp.float32)

    stacked = jnp.stack([project(history[slot_index]) for slot_index in range(HIST)])
    gathered = lax.all_gather(stacked, "src", axis=2, tiled=True)
    past = [gathered[slot_index] for slot_index in range(HIST)]
    results = []
    latest = None
    for step in range(STEPS):
        if step > 0:
            newest = lax.all_gather(latest, "src", axis=1, tiled=True)
            past = past[1:] + [newest]
        partial_value = couple(past[-1], 1) + couple(past[-2], 2) + couple(past[-3], 3)
        field = lax.psum_scatter(
            partial_value.astype(jnp.bfloat16), "obs", scatter_dimension=1, tiled=True
        )
        field_cast = field.reshape(excite, local_clusters, rank)
        far_field = jnp.einsum(
            "ecr,crb->ceb", field_cast, expand_basis, preferred_element_type=jnp.float32
        )
        residual_field = (incident[step].astype(jnp.float32) - far_field).astype(jnp.bfloat16)
        current = jnp.einsum(
            "ceb,cbd->ced", residual_field, near_inverse, preferred_element_type=jnp.float32
        ).astype(jnp.bfloat16)
        results.append(current)
        if step + 1 < STEPS:
            latest = project(current)
    return jnp.stack(results)


def solution(mesh):
    placed = (
        P(None, ("obs", "src"), None, None),
        P(None, ("obs", "src"), None, None),
        P(("obs", "src"), None, None),
        P(("obs", "src"), None, None),
        P(("obs", "src"), None, None),
        P(None, "obs", None, "src", None),
        P("obs", None, "src", None),
    )
    return jax.shard_map(
        per_device,
        mesh=mesh,
        in_specs=placed,
        out_specs=P(None, ("obs", "src"), None, None),
        check_vma=False,
    )
```

profile of v0, /device:TPU:0, one launch (start us, length us, event | category | flops | bytes accessed | tf_op | source)
XLA Modules:
  0.0 237.1 jit_solution(1757093044412803134)
XLA Ops:
  6.5 1.4 convolution_convert_fusion.11
  8.0 1.4 convolution_convert_fusion.10
  9.3 1.4 convolution_convert_fusion.9
  11.1 2.3 fusion.46
  13.3 2.0 squeeze.40
  15.3 1.8 squeeze.42
  17.2 4.3 %select_select_fusion = (bf16[16,64,8,64]{3,2,1,0:T(8,128)(2,1)}, bf16[16,64,8,64]{3,2,1,0:T(8,128)(2,1)}, bf16[16,64,8,64]{3,2,1,0:T(8,128)(2,1)}) fusion(bf16[16,64,8,64]{3,2,1,0:T(8,128)(2,1)} %squeeze.42, bf16[16,64,8,64]{3,2,1,0:T(8,128)(2,1)} %squeeze.40, pred[16,8]{1,0:T(8,128)(4,1)S(1)} %copy.20, pred[16,8]{1,0:T(8,128)(4,1)S(1)} %copy.19, ...), kind=kLoop, calls=%fused_computation.17 | loop fusion | flops 2621440 | bytes 5243264 | tf_op jit(solution)/shard_map/jit(_where)/select_n | solution.py:27
  21.5 4.0 %select_n.97 = bf16[1024,512]{1,0:T(8,128)(2,1)} reshape(bf16[16,64,8,64]{3,2,1,0:T(8,128)(2,1)} %get-tuple-element.7) | data formatting | bytes 2097152 | tf_op jit(solution)/shard_map/jit(_where)/select_n | solution.py:27
  25.6 11.9 %all_gather.15 = bf16[3,64,1024]{1,2,0:T(8,128)(2,1)S(1)} all-gather(bf16[3,64,128]{1,2,0:T(8,128)(2,1)S(1)} %pad_maximum_fusion), channel_id=1, replica_groups=mesh['obs'=4,'src'=8] {'src'}, dimensions={2}, use_global_device_ids=true | all-gather | bytes 442368 | tf_op jit(solution)/shard_map/all_gather | solution.py:40
  37.5 3.5 %select_n.100 = bf16[1024,512]{1,0:T(8,128)(2,1)S(1)} reshape(bf16[16,64,8,64]{3,2,1,0:T(8,128)(2,1)} %get-tuple-element.6) | data formatting | bytes 2097152 | tf_op jit(solution)/shard_map/jit(_where)/select_n | solution.py:27
  41.0 3.2 %select_n.103 = bf16[1024,512]{1,0:T(8,128)(2,1)S(1)} reshape(bf16[16,64,8,64]{3,2,1,0:T(8,128)(2,1)} %get-tuple-element.5) | data formatting | bytes 2097152 | tf_op jit(solution)/shard_map/jit(_where)/select_n | solution.py:27
  44.2 1.5 fusion.42
  45.7 0.3 convolution_add_fusion.7
  46.0 0.3 fusion.11
  46.3 0.8 copy.30
  47.2 1.0 fusion.39
  48.2 0.3 broadcast_in_dim.35
  48.5 2.7 %broadcast_in_dim.38 = pred[1024,512]{1,0:T(32,128)(4,1)} reshape(pred[16,64,8,64]{3,2,1,0:T(8,128)(4,1)S(1)} %broadcast_in_dim.35) | data formatting | bytes 1048576 | tf_op jit(solution)/shard_map/jit(_where)/broadcast_in_dim | solution.py:27
  51.2 0.3 broadcast_in_dim.36
  51.6 2.7 %broadcast_in_dim.39 = pred[1024,512]{1,0:T(32,128)(4,1)} reshape(pred[16,64,8,64]{3,2,1,0:T(8,128)(4,1)S(1)} %broadcast_in_dim.36) | data formatting | bytes 1048576 | tf_op jit(solution)/shard_map/jit(_where)/broadcast_in_dim | solution.py:27
  54.3 2.5 %bitcast_select_fusion.1 = bf16[1024,512]{1,0:T(8,128)(2,1)S(1)} fusion(pred[1024,512]{1,0:T(32,128)(4,1)} %broadcast_in_dim.38, pred[1024,512]{1,0:T(32,128)(4,1)} %broadcast_in_dim.39, bf16[128,8,4,128]{3,2,1,0:T(4,128)(2,1)} %bitcast.199, bf16[128,8,4,128]{3,2,1,0:T(4,128)(2,1)} %bitcast.202), kind=kLoop, calls=%fused_computation.47 | loop fusion | flops 1048576 | bytes 4194304 | tf_op jit(solution)/shard_map/jit(_where)/select_n | solution.py:27
  56.8 1.9 fusion.41
  58.8 8.2 %reduce-scatter.16.cloned.1.call-done = bf16[128,64]{1,0:T(8,128)(2,1)} async-done(((bf16[512,64]{1,0:T(8,128)(2,1)}), bf16[128,64]{1,0:T(8,128)(2,1)}) %reduce-scatter.16.cloned.1.call-update) | async-done | bytes 16400
  67.0 6.7 %bitcast_dynamic-update-slice_fusion.3 = (bf16[5,2,64,1536]{3,2,1,0:T(8,128)(2,1)}, bf16[2,64,1536]{2,1,0:T(8,128)(2,1)}) fusion(bf16[2,1536,1536]{2,1,0:T(8,128)(2,1)} %param.11, bf16[64,2,64]{0,2,1:T(8,128)(2,1)} %bitcast.214, bf16[2,64,1536]{2,1,0:T(8,128)(2,1)S(1)} %copy-done, bf16[5,2,64,1536]{3,2,1,0:T(8,128)(2,1)} %param.8), kind=kOutput, calls=%fused_computation.64 | convolution fusion | flops 629932032 | bytes 11042816 | tf_op jit(solution)/shard_map/ceb,cbd->ced/dot_general | solution.py:57
  73.8 1.4 fusion.14
  75.1 0.6 copy.22
  75.8 0.8 reshape.176
  76.6 9.2 %all_gather.16 = bf16[64,1024]{1,0:T(8,128)(2,1)S(1)} all-gather(bf16[64,128]{1,0:T(8,128)(2,1)S(1)} %reshape.176), channel_id=1, replica_groups=mesh['obs'=4,'src'=8] {'src'}, dimensions={1}, use_global_device_ids=true | all-gather | bytes 147456 | tf_op jit(solution)/shard_map/all_gather | solution.py:46
  85.8 0.6 copy-done.12
  86.5 2.3 fusion.13
  88.7 1.6 copy.32
  90.4 1.9 fusion.40
  92.3 14.9 %reduce-scatter.18.cloned.1.call-done = bf16[128,64]{1,0:T(8,128)(2,1)} async-done(((bf16[512,64]{1,0:T(8,128)(2,1)}), bf16[128,64]{1,0:T(8,128)(2,1)}) %reduce-scatter.18.cloned.1.call-update) | async-done | bytes 16400
  107.2 6.7 %bitcast_dynamic-update-slice_fusion.2 = (bf16[5,2,64,1536]{3,2,1,0:T(8,128)(2,1)}, bf16[2,64,1536]{2,1,0:T(8,128)(2,1)}) fusion(bf16[5,2,64,1536]{3,2,1,0:T(8,128)(2,1)} %get-tuple-element.13, bf16[2,1536,1536]{2,1,0:T(8,128)(2,1)} %param.11, bf16[64,2,64]{0,2,1:T(8,128)(2,1)} %bitcast.216, bf16[2,64,1536]{2,1,0:T(8,128)(2,1)S(1)} %copy-done, ...), kind=kOutput, calls=%fused_computation.63 | convolution fusion | flops 629932032 | bytes 11042816 | tf_op jit(solution)/shard_map/ceb,cbd->ced/dot_general | solution.py:57
  114.0 1.3 fusion.15
  115.3 0.6 copy.24
  115.9 0.8 reshape.178
  116.7 9.1 %all_gather.17 = bf16[64,1024]{1,0:T(8,128)(2,1)S(1)} all-gather(bf16[64,128]{1,0:T(8,128)(2,1)S(1)} %reshape.178), channel_id=1, replica_groups=mesh['obs'=4,'src'=8] {'src'}, dimensions={1}, use_global_device_ids=true | all-gather | bytes 147456 | tf_op jit(solution)/shard_map/all_gather | solution.py:46
  125.9 0.5 fusion.45
  126.8 0.8 copy.34
  127.7 1.3 broadcast_in_dim.37
  129.0 4.0 %broadcast_in_dim.40 = pred[1024,512]{1,0:T(32,128)(4,1)} reshape(pred[16,64,8,64]{3,2,1,0:T(8,128)(4,1)} %broadcast_in_dim.37) | data formatting | bytes 1048576 | tf_op jit(solution)/shard_map/jit(_where)/broadcast_in_dim | solution.py:27
  133.0 11.5 %reduce-scatter.20.cloned.1.call-done = bf16[128,64]{1,0:T(8,128)(2,1)} async-done(((bf16[512,64]{1,0:T(8,128)(2,1)}), bf16[128,64]{1,0:T(8,128)(2,1)}) %reduce-scatter.20.cloned.1.call-update) | async-done | bytes 16400
  144.5 6.6 %bitcast_dynamic-update-slice_fusion.1 = (bf16[5,2,64,1536]{3,2,1,0:T(8,128)(2,1)}, bf16[2,64,1536]{2,1,0:T(8,128)(2,1)S(1)}) fusion(bf16[5,2,64,1536]{3,2,1,0:T(8,128)(2,1)} %get-tuple-element.15, bf16[2,1536,1536]{2,1,0:T(8,128)(2,1)} %param.11, bf16[64,2,64]{0,2,1:T(8,128)(2,1)} %bitcast.215, bf16[2,64,1536]{2,1,0:T(8,128)(2,1)S(1)} %copy-done, ...), kind=kOutput, calls=%fused_computation.62 | convolution fusion | flops 629932032 | bytes 11042816 | tf_op jit(solution)/shard_map/ceb,cbd->ced/dot_general | solution.py:57
  151.3 0.6 copy.26
  152.0 0.9 reshape.180
  152.9 9.1 %all_gather.18 = bf16[64,1024]{1,0:T(8,128)(2,1)S(1)} all-gather(bf16[64,128]{1,0:T(8,128)(2,1)S(1)} %reshape.180), channel_id=1, replica_groups=mesh['obs'=4,'src'=8] {'src'}, dimensions={1}, use_global_device_ids=true | all-gather | bytes 147456 | tf_op jit(solution)/shard_map/all_gather | solution.py:46
  162.1 0.7 copy-done.19
  162.7 1.6 fusion.44
  164.3 0.3 convolution_add_fusion.3
  164.7 1.5 fusion.9
  166.1 1.6 copy.36
  167.8 16.8 %reduce-scatter.22.cloned.1.call-done = bf16[128,64]{1,0:T(8,128)(2,1)} async-done(((bf16[512,64]{1,0:T(8,128)(2,1)}), bf16[128,64]{1,0:T(8,128)(2,1)}) %reduce-scatter.22.cloned.1.call-update) | async-done | bytes 16400
  184.6 6.7 %bitcast_dynamic-update-slice_fusion = (bf16[5,2,64,1536]{3,2,1,0:T(8,128)(2,1)}, bf16[2,64,1536]{2,1,0:T(8,128)(2,1)}) fusion(bf16[5,2,64,1536]{3,2,1,0:T(8,128)(2,1)} %get-tuple-element.17, bf16[2,1536,1536]{2,1,0:T(8,128)(2,1)} %param.11, bf16[64,2,64]{0,2,1:T(8,128)(2,1)} %bitcast.217, bf16[2,64,1536]{2,1,0:T(8,128)(2,1)S(1)} %copy-done, ...), kind=kOutput, calls=%fused_computation.61 | convolution fusion | flops 629932032 | bytes 11042816 | tf_op jit(solution)/shard_map/ceb,cbd->ced/dot_general | solution.py:57
  191.3 1.4 fusion.17
  192.7 0.6 copy.28
  193.3 0.8 reshape.182
  194.2 9.4 %all_gather.19 = bf16[64,1024]{1,0:T(8,128)(2,1)S(1)} all-gather(bf16[64,128]{1,0:T(8,128)(2,1)S(1)} %reshape.182), channel_id=1, replica_groups=mesh['obs'=4,'src'=8] {'src'}, dimensions={1}, use_global_device_ids=true | all-gather | bytes 147456 | tf_op jit(solution)/shard_map/all_gather | solution.py:46
  203.6 1.6 fusion.43
  205.2 0.3 convolution_add_fusion.1
  205.5 0.8 fusion.10
  206.4 0.8 copy.38
  207.1 16.9 %reduce-scatter.24.cloned.1.call-done = bf16[128,64]{1,0:T(8,128)(2,1)} async-done(((bf16[512,64]{1,0:T(8,128)(2,1)}), bf16[128,64]{1,0:T(8,128)(2,1)}) %reduce-scatter.24.cloned.1.call-update) | async-done | bytes 16400
  224.0 6.6 %fusion.6 = bf16[5,2,64,1536]{3,2,1,0:T(8,128)(2,1)} fusion(bf16[5,2,64,1536]{3,2,1,0:T(8,128)(2,1)} %get-tuple-element.19, bf16[2,1536,1536]{2,1,0:T(8,128)(2,1)} %param.11, bf16[64,2,64]{0,2,1:T(8,128)(2,1)} %bitcast.218, bf16[2,64,1536]{2,1,0:T(8,128)(2,1)S(1)} %copy-done, bf16[5,2,64,1536]{3,2,1,0:T(8,128)(2,1)} %param.8), kind=kOutput, calls=%fused_computation.16 | convolution fusion | flops 629932032 | bytes 10649600 | tf_op jit(solution)/shard_map/ceb,cbd->ced/dot_general | solution.py:57
  (66 shorter events, 1.4 us)
Async XLA Ops:
  6.5 60.5 %copy-start = (bf16[2,64,1536]{2,1,0:T(8,128)(2,1)S(1)}, bf16[2,64,1536]{2,1,0:T(8,128)(2,1)}, u32[]{:S(2)}) copy-start(bf16[2,64,1536]{2,1,0:T(8,128)(2,1)} %param.10) | copy-start | bytes 1179652
  6.5 4.2 %copy-start.23 = (s32[16,4,1,2]{0,3,2,1:T(2,128)S(1)}, s32[16,4,1,2]{0,3,2,1:T(2,128)}, u32[]{:S(2)}) copy-start(s32[16,4,1,2]{0,3,2,1:T(2,128)} %param.13) | copy-start | bytes 1540
  6.5 60.5 %reduce-scatter.16.cloned.1.call-start = ((), (), s32[]{:S(2)}) async-start(), calls=%async_computation.5 | async-start | bytes 163840
  11.1 6.1 %copy-start.21 = (pred[16,8]{1,0:T(8,128)(4,1)}, pred[16,8]{1,0:T(8,128)(4,1)S(1)}, u32[]{:S(2)}) copy-start(pred[16,8]{1,0:T(8,128)(4,1)S(1)} %copy.20) | copy-start | bytes 388
  13.3 3.8 %copy-start.1 = (bf16[1,1024,4,1,128]{4,2,3,1,0:T(4,128)(2,1)}, bf16[1,1024,4,1,128]{4,2,3,1,0:T(4,128)(2,1)S(1)}, u32[]{:S(2)}) copy-start(bf16[1,1024,4,1,128]{4,2,3,1,0:T(4,128)(2,1)S(1)} %get-tuple-element.8) | copy-start | bytes 3145732
  13.3 3.8 %copy-start.3 = (bf16[1,1024,4,1,128]{4,2,3,1,0:T(4,128)(2,1)}, bf16[1,1024,4,1,128]{4,2,3,1,0:T(4,128)(2,1)S(1)}, u32[]{:S(2)}) copy-start(bf16[1,1024,4,1,128]{4,2,3,1,0:T(4,128)(2,1)S(1)} %get-tuple-element.9) | copy-start | bytes 3145732
  37.5 9.7 %copy-start.5 = (bf16[3,64,1024]{1,2,0:T(8,128)(2,1)}, bf16[3,64,1024]{1,2,0:T(8,128)(2,1)S(1)}, u32[]{:S(2)}) copy-start(bf16[3,64,1024]{1,2,0:T(8,128)(2,1)S(1)} %all_gather.15) | copy-start | bytes 1179652
  47.1 60.1 %reduce-scatter.18.cloned.1.call-start = ((), (), s32[]{:S(2)}) async-start(), calls=%async_computation.6 | async-start | bytes 163840
  67.0 19.4 %copy-start.4 = (bf16[1,1024,4,1,128]{4,2,3,1,0:T(4,128)(2,1)S(1)}, bf16[1,1024,4,1,128]{4,2,3,1,0:T(4,128)(2,1)}, u32[]{:S(2)}) copy-start(bf16[1,1024,4,1,128]{4,2,3,1,0:T(4,128)(2,1)} %copy-done.3) | copy-start | bytes 3145732
  85.8 0.6 copy-start.12
  90.4 54.2 %reduce-scatter.20.cloned.1.call-start = ((), (), s32[]{:S(2)}) async-start(), calls=%async_computation.7 | async-start | bytes 163840
  107.2 6.8 %copy-start.6 = (bf16[2,64,1536]{2,1,0:T(8,128)(2,1)S(1)}, bf16[2,64,1536]{2,1,0:T(8,128)(2,1)}, u32[]{:S(2)}) copy-start(bf16[2,64,1536]{2,1,0:T(8,128)(2,1)} %param.9) | copy-start | bytes 1179652
  107.2 18.7 %copy-start.9 = (pred[1024,512]{1,0:T(32,128)(4,1)S(1)}, pred[1024,512]{1,0:T(32,128)(4,1)}, u32[]{:S(2)}) copy-start(pred[1024,512]{1,0:T(32,128)(4,1)} %broadcast_in_dim.38) | copy-start | bytes 1572868
  114.0 12.6 %copy-start.13 = (bf16[64,1024]{1,0:T(8,128)(2,1)S(1)}, bf16[64,1024]{1,0:T(8,128)(2,1)}, u32[]{:S(2)}) copy-start(bf16[64,1024]{1,0:T(8,128)(2,1)} %copy-done.12) | copy-start | bytes 393220
  116.7 9.8 %copy-start.15 = (f32[64,512]{1,0:T(8,128)S(1)}, f32[64,512]{1,0:T(8,128)}, u32[]{:S(2)}) copy-start(f32[64,512]{1,0:T(8,128)} %fusion.40) | copy-start | bytes 393220
  125.9 0.7 copy-start.16
  125.9 1.8 copy-start.22
  127.6 57.0 %reduce-scatter.22.cloned.1.call-start = ((), (), s32[]{:S(2)}) async-start(), calls=%async_computation.8 | async-start | bytes 163840
  152.0 12.7 %copy-start.2 = (bf16[1,1024,4,1,128]{4,2,3,1,0:T(4,128)(2,1)S(1)}, bf16[1,1024,4,1,128]{4,2,3,1,0:T(4,128)(2,1)}, u32[]{:S(2)}) copy-start(bf16[1,1024,4,1,128]{4,2,3,1,0:T(4,128)(2,1)} %copy-done.1) | copy-start | bytes 3145732
  152.9 11.4 %copy-start.17 = (bf16[64,1024]{1,0:T(8,128)(2,1)S(1)}, bf16[64,1024]{1,0:T(8,128)(2,1)}, u32[]{:S(2)}) copy-start(bf16[64,1024]{1,0:T(8,128)(2,1)} %copy-done.16) | copy-start | bytes 393220
  152.9 11.7 %copy-start.7 = (pred[1024,512]{1,0:T(32,128)(4,1)S(1)}, pred[1024,512]{1,0:T(32,128)(4,1)}, u32[]{:S(2)}) copy-start(pred[1024,512]{1,0:T(32,128)(4,1)} %broadcast_in_dim.39) | copy-start | bytes 1572868
  152.9 11.7 %copy-start.10 = (pred[1024,512]{1,0:T(32,128)(4,1)S(1)}, pred[1024,512]{1,0:T(32,128)(4,1)}, u32[]{:S(2)}) copy-start(pred[1024,512]{1,0:T(32,128)(4,1)} %broadcast_in_dim.40) | copy-start | bytes 1572868
  152.9 11.7 %copy-start.14 = (bf16[64,1024]{1,0:T(8,128)(2,1)S(1)}, bf16[64,1024]{1,0:T(8,128)(2,1)}, u32[]{:S(2)}) copy-start(bf16[64,1024]{1,0:T(8,128)(2,1)} %copy-done.12) | copy-start | bytes 393220
  162.1 0.7 copy-start.19
  167.8 56.2 %reduce-scatter.24.cloned.1.call-start = ((), (), s32[]{:S(2)}) async-start(), calls=%async_computation.9 | async-start | bytes 163840
  194.1 11.0 %copy-start.20 = (bf16[64,1024]{1,0:T(8,128)(2,1)S(1)}, bf16[64,1024]{1,0:T(8,128)(2,1)}, u32[]{:S(2)}) copy-start(bf16[64,1024]{1,0:T(8,128)(2,1)} %copy-done.19) | copy-start | bytes 393220
  194.1 11.3 %copy-start.8 = (pred[1024,512]{1,0:T(32,128)(4,1)S(1)}, pred[1024,512]{1,0:T(32,128)(4,1)}, u32[]{:S(2)}) copy-start(pred[1024,512]{1,0:T(32,128)(4,1)} %broadcast_in_dim.39) | copy-start | bytes 1572868
  194.2 11.3 %copy-start.11 = (pred[1024,512]{1,0:T(32,128)(4,1)S(1)}, pred[1024,512]{1,0:T(32,128)(4,1)}, u32[]{:S(2)}) copy-start(pred[1024,512]{1,0:T(32,128)(4,1)} %broadcast_in_dim.40) | copy-start | bytes 1572868
  194.2 11.3 %copy-start.18 = (bf16[64,1024]{1,0:T(8,128)(2,1)S(1)}, bf16[64,1024]{1,0:T(8,128)(2,1)}, u32[]{:S(2)}) copy-start(bf16[64,1024]{1,0:T(8,128)(2,1)} %copy-done.16) | copy-start | bytes 393220
Sparse Core Ops, SparseCore 0:
  47.3 19.7 reduce-scatter.15
  90.5 16.6 reduce-scatter.17
  127.7 16.7 reduce-scatter.19
  167.9 16.6 reduce-scatter.21
  207.3 16.6 reduce-scatter.23
where the time goes:
time: 238 us; the launch traced here: 237 us
  waiting for transfers between devices  68.4 us (29%)
  matrix products  57.8 us (24%)
  blocking collectives  48.8 us (21%)
  local copies, waits for them, and re-layouts  41.5 us (17%)
  between operations  13.5 us (6%)
  other arithmetic  6.91 us (3%)
    unnamed x10, waiting for transfers between devices  68.4 us
    all_gather x4, blocking collectives, per_device(): newest = lax.all_gather(latest, 'src', axis=1, tiled=True)  36.9 us
    dot_general x5, matrix products, per_device(): jnp.einsum('ceb,cbd->ced', residual_field, near_inverse, preferred_elemen...  33.3 us
    dot_general x15, matrix products, couple(): jnp.dot(columns, matrices[delay - 1], preferred_element_type=jnp.float32)  16.1 us
    all_gather x1, blocking collectives, per_device(): gathered = lax.all_gather(stacked, 'src', axis=2, tiled=True)  11.9 us
    broadcast_in_dim x6, local copies, waits for them, and re-layouts, per_device(): combined = jnp.where(chosen, kernel[tap_index], combined)  11.4 us
    select_n x3, local copies, waits for them, and re-layouts, per_device(): combined = jnp.where(chosen, kernel[tap_index], combined)  10.7 us
    dot_general x7, matrix products, project(): jnp.einsum('ceb,crb->ecr', current, proj_basis, preferred_element_type=jn...  8.37 us
  transfers between devices with their start and end apart: 5, of which 5 were waited for; matrix products, arithmetic and copies ran while one was open for 8% of the time, Pallas kernels for 0%

commit v1 on v0

v1 whole, which is shorter than its diff:
```python
import functools

import jax
import jax.numpy as jnp
from jax import lax
from jax.experimental import pallas as pl
from jax.experimental.pallas import tpu as pltpu
from jax.sharding import PartitionSpec as P

MESH = pl.DeviceIdType.MESH
F32 = jnp.float32
BF16 = jnp.bfloat16
NT = (((1,), (1,)), ((), ()))


def flipped(me, bits, count):
    other = me
    place = 1
    while place < count:
        if bits & place:
            other = other + (1 - 2 * ((me // place) % 2)) * place
        place *= 2
    return other


def partner(me, turn, count):
    if count & (count - 1) == 0:
        return flipped(me, count - turn, count)
    return lax.rem(me + turn, count)


def kernel(n_obs, n_src, hist_ref, inc_ref, proj_ref, expand_ref, near_ref, coup_ref, lag_ref, out_ref,
           hv, av, pv, nv, cv, cf, wv, yv, xn, bv, mv, qh, qn, sendp, recvp, base, ov,
           load_sem, out_sem, hs_sem, hr_sem, qs_sem, qr_sem, ps_sem, pr_sem):
    o = lax.axis_index("obs")
    s = lax.axis_index("src")
    hist, clusters, excite, unknowns = hist_ref.shape
    steps = inc_ref.shape[0]
    rank = proj_ref.shape[1]
    width = clusters * rank
    sources = lag_ref.shape[2]
    tile = 256

    loads = []

    def load(src, dst):
        copy = pltpu.make_async_copy(src, dst, load_sem.at[len(loads)])
        copy.start()
        loads.append(copy)
        return copy

    def rows(index, size):
        return pl.ds(index * size, size)

    h_loads = [load(proj_ref.at[c], pv.at[c, rows(c, rank)]) for c in range(clusters)]
    h_loads += [load(hist_ref.at[k, c], hv.at[c, rows(k, excite)]) for c in range(clusters) for k in range(hist)]
    c_loads = [load(coup_ref, cv)]
    n_loads = []
    for c in range(clusters):
        mine = [load(inc_ref.at[t, c], av.at[c, rows(t, excite)]) for t in range(steps)]
        mine.append(load(expand_ref.at[c], av.at[c, rows(steps, excite)]))
        mine.append(load(near_ref.at[c], nv.at[c]))
        n_loads.append(mine)

    barrier = pltpu.get_barrier_semaphore()
    src_peers = [partner(s, turn, n_src) for turn in range(1, n_src)]
    obs_peers = [partner(o, turn, n_obs) for turn in range(1, n_obs)]
    for peer in src_peers:
        pl.semaphore_signal(barrier, inc=1, device_id=(o, peer), device_id_type=MESH)
    for peer in obs_peers:
        pl.semaphore_signal(barrier, inc=1, device_id=(peer, s), device_id_type=MESH)

    for c in range(clusters):
        for k in range(clusters):
            if k != c:
                pv[c, k * rank:(k + 1) * rank] = jnp.zeros((rank, unknowns), BF16)
                xn[c, k * rank:(k + 1) * rank] = jnp.zeros((rank, unknowns), BF16)

    for copy in h_loads:
        copy.wait()
    past = jnp.zeros((hist * excite, width), F32)
    for c in range(clusters):
        past = past + lax.dot_general(hv[c], pv[c], NT, preferred_element_type=F32)
    qh[s] = past.astype(BF16)
    pl.semaphore_wait(barrier, n_src + n_obs - 2)

    def h_copy(turn, slot):
        return pltpu.make_async_remote_copy(
            src_ref=qh.at[slot], dst_ref=qh.at[slot], send_sem=hs_sem.at[turn], recv_sem=hr_sem.at[slot],
            device_id=(o, src_peers[turn]), device_id_type=MESH)

    def q_copy(step, turn, slot):
        return pltpu.make_async_remote_copy(
            src_ref=qn.at[step, slot], dst_ref=qn.at[step, slot], send_sem=qs_sem.at[step, turn],
            recv_sem=qr_sem.at[step, slot], device_id=(o, src_peers[turn]), device_id_type=MESH)

    def p_copy(step, turn, at, slot):
        return pltpu.make_async_remote_copy(
            src_ref=sendp.at[step, at], dst_ref=recvp.at[step, slot], send_sem=ps_sem.at[step, turn],
            recv_sem=pr_sem.at[step, slot], device_id=(obs_peers[turn], s), device_id_type=MESH)

    for turn in range(n_src - 1):
        h_copy(turn, s).start()

    for copy in c_loads:
        copy.wait()
    lane = lax.broadcasted_iota(jnp.int32, (rank, width), 1)

    def build(j, carry):
        for p in range(2):
            cf[p] = cv[p, pl.ds(pl.multiple_of(j * (rank * n_obs), rank * n_obs), rank * n_obs), :].astype(F32)
        at = pl.ds(pl.multiple_of(j * rank, rank), rank)
        for to in range(n_obs):
            lag = jnp.full((rank, width), lag_ref[to, 0, j], jnp.int32)
            for k in range(1, clusters):
                lag = jnp.where(lane >= k * rank, lag_ref[to, k, j], lag)
            first = cf[0, pl.ds(to, rank, stride=n_obs), :]
            second = cf[1, pl.ds(to, rank, stride=n_obs), :]
            zero = jnp.zeros_like(first)
            one, two = lag == 1, lag == 2
            cols = slice(to * width, (to + 1) * width)
            wv[0, at, cols] = jnp.where(one, first, zero).astype(BF16)
            wv[1, at, cols] = jnp.where(two, first, jnp.where(one, second, zero)).astype(BF16)
            wv[2, at, cols] = jnp.where(two, second, zero).astype(BF16)
        return carry

    lax.fori_loop(0, sources, build, 0)

    def near(c):
        for copy in n_loads[c]:
            copy.wait()

        def column(j, carry):
            at = pl.ds(pl.multiple_of(j * tile, tile), tile)
            value = jnp.dot(av[c], nv[c, :, at], preferred_element_type=F32)
            yv[c, :, at] = value
            xn[c, c * rank:(c + 1) * rank, at] = value[steps * excite:].astype(BF16)
            return carry

        lax.fori_loop(0, unknowns // tile, column, 0)
        return lax.dot_general(yv[c].astype(BF16), pv[c], NT, preferred_element_type=F32)

    def keep(c, value):
        if c == 0:
            bv[...] = value[:steps * excite]
        else:
            bv[...] += value[:steps * excite]
        mv[c * rank:(c + 1) * rank] = value[steps * excite:].astype(BF16)

    keep(0, near(0))

    for turn in range(n_src - 1):
        h_copy(turn, src_peers[turn]).wait_recv()

    def gathered(ref):
        return jnp.concatenate([ref[k] for k in range(n_src)], axis=1)

    def slot_of(ref, k):
        return jnp.concatenate([ref[j, k * excite:(k + 1) * excite] for j in range(n_src)], axis=1)

    older = [slot_of(qh, k) for k in range(hist)]

    def send_partial(step, total):
        for to in range(n_obs):
            sendp[step, to] = total[:, to * width:(to + 1) * width].astype(BF16)
        for turn in range(n_obs - 1):
            p_copy(step, turn, obs_peers[turn], o).start()

    total = jnp.dot(older[hist - 1], wv[0], preferred_element_type=F32)
    for d in range(2, hist + 1):
        total = total + jnp.dot(older[hist - d], wv[d - 1], preferred_element_type=F32)
    send_partial(0, total)

    for ahead in range(1, hist):
        total = None
        for d in range(ahead + 1, hist + 1):
            term = jnp.dot(older[hist + ahead - d], wv[d - 1], preferred_element_type=F32)
            total = term if total is None else total + term
        base[ahead] = total
    for ahead in range(hist, steps):
        base[ahead] = jnp.zeros((excite, n_obs * width), F32)

    for c in range(1, clusters):
        keep(c, near(c))

    outs = []

    def finish(step, field):
        for c in range(clusters):
            far = jnp.dot(field, xn[c], preferred_element_type=F32)
            ov[step, c] = (yv[c, step * excite:(step + 1) * excite] - far).astype(BF16)
            copy = pltpu.make_async_copy(ov.at[step, c], out_ref.at[step, c], out_sem.at[step, c])
            copy.start()
            outs.append(copy)

    for step in range(steps):
        field = sendp[step, o].astype(F32)
        for turn in range(n_obs - 1):
            p_copy(step, turn, 0, obs_peers[turn]).wait_recv()
            field = field + recvp[step, obs_peers[turn]].astype(F32)
        field = field.astype(BF16)
        if step + 1 == steps:
            finish(step, field)
            break
        newest = bv[step * excite:(step + 1) * excite] - jnp.dot(field, mv[...], preferred_element_type=F32)
        qn[step, s] = newest.astype(BF16)
        for turn in range(n_src - 1):
            q_copy(step, turn, s).start()
        finish(step, field)
        for turn in range(n_src - 1):
            q_copy(step, turn, src_peers[turn]).wait_recv()
        columns = gathered(qn.at[step])
        send_partial(step + 1, base[step + 1] + jnp.dot(columns, wv[0], preferred_element_type=F32))
        for d in range(2, hist + 1):
            if step + d < steps:
                base[step + d] += jnp.dot(columns, wv[d - 1], preferred_element_type=F32)

    for copy in outs:
        copy.wait()
    for turn in range(n_src - 1):
        h_copy(turn, s).wait_send()
    for step in range(steps):
        for turn in range(n_obs - 1):
            p_copy(step, turn, obs_peers[turn], o).wait_send()
        if step + 1 < steps:
            for turn in range(n_src - 1):
                q_copy(step, turn, s).wait_send()


def per_device(n_obs, n_src, history, incident, proj_basis, expand_basis, near_inverse, couplings, lags):
    hist, clusters, excite, unknowns = history.shape
    steps = incident.shape[0]
    rank = proj_basis.shape[1]
    width = clusters * rank
    taps, src_rows = couplings.shape[:2]
    sources = lags.shape[0]
    obs_cols = n_obs * width
    flat = couplings.reshape(taps, src_rows * n_obs, width)
    lag_table = jnp.transpose(lags.reshape(sources, n_obs, clusters), (1, 2, 0))
    stacked = (steps + 1) * excite
    loads = clusters * (1 + hist + steps + 2) + 1
    any_spec = pl.BlockSpec(memory_space=pl.ANY)
    dma = pltpu.SemaphoreType.DMA
    return pl.pallas_call(
        functools.partial(kernel, n_obs, n_src),
        out_shape=jax.ShapeDtypeStruct(incident.shape, BF16),
        in_specs=[any_spec] * 6 + [pl.BlockSpec(memory_space=pltpu.SMEM)],
        out_specs=any_spec,
        scratch_shapes=[
            pltpu.VMEM((clusters, hist * excite, unknowns), BF16),
            pltpu.VMEM((clusters, stacked, unknowns), BF16),
            pltpu.VMEM((clusters, width, unknowns), BF16),
            pltpu.VMEM((clusters, unknowns, unknowns), BF16),
            pltpu.VMEM((taps, src_rows * n_obs, width), BF16),
            pltpu.VMEM((taps, rank * n_obs, width), F32),
            pltpu.VMEM((hist, src_rows, obs_cols), BF16),
            pltpu.VMEM((clusters, stacked, unknowns), F32),
            pltpu.VMEM((clusters, width, unknowns), BF16),
            pltpu.VMEM((steps * excite, width), F32),
            pltpu.VMEM((width, width), BF16),
            pltpu.VMEM((n_src, hist * excite, width), BF16),
            pltpu.VMEM((steps - 1, n_src, excite, width), BF16),
            pltpu.VMEM((steps, n_obs, excite, width), BF16),
            pltpu.VMEM((steps, n_obs, excite, width), BF16),
            pltpu.VMEM((steps, excite, obs_cols), F32),
            pltpu.VMEM((steps, clusters, excite, unknowns), BF16),
            dma((loads,)),
            dma((steps, clusters)),
            dma((n_src,)),
            dma((n_src,)),
            dma((steps - 1, n_src)),
            dma((steps - 1, n_src)),
            dma((steps, n_obs)),
            dma((steps, n_obs)),
        ],
        compiler_params=pltpu.CompilerParams(
            collective_id=0, has_side_effects=True, vmem_limit_bytes=63000 * 1024
        ),
    )(history, incident, proj_basis, expand_basis, near_inverse, flat, lag_table)


def solution(mesh):
    placed = (
        P(None, ("obs", "src"), None, None),
        P(None, ("obs", "src"), None, None),
        P(("obs", "src"), None, None),
        P(("obs", "src"), None, None),
        P(("obs", "src"), None, None),
        P(None, "obs", None, "src", None),
        P("obs", None, "src", None),
    )
    return jax.shard_map(
        functools.partial(per_device, mesh.shape["obs"], mesh.shape["src"]),
        mesh=mesh,
        in_specs=placed,
        out_specs=P(None, ("obs", "src"), None, None),
        check_vma=False,
    )
```

time: 238 us -> 53.2 us (0.22)
  waiting for transfers between devices: 68.4 us -> 0 us
  matrix products: 57.8 us -> 0 us
  Pallas kernels: 0 us -> 50.1 us
  blocking collectives: 48.8 us -> 0 us
  local copies, waits for them, and re-layouts: 41.5 us -> 2.94 us
  between operations: 13.5 us -> 0.01 us
  other arithmetic: 6.91 us -> 0 us
    unnamed x10 -> x0, waiting for transfers between devices: 68.4 us -> none
    dot_general x27 -> x0, matrix products: 57.8 us -> none  [the longest x5 33.3 us: per_device(): jnp.einsum('ceb,cbd->ced', residual_field, near_inverse, preferred_elemen...]
    pallas_call x0 -> x1, Pallas kernels: none -> 50.1 us  [per_device(): pl.pallas_call(functools.partial(kernel, n_obs, n_src), out_shape=jax.Sha...]
    all_gather x5 -> x0, blocking collectives: 48.8 us -> none  [the longest x4 36.9 us: per_device(): newest = lax.all_gather(latest, 'src', axis=1, tiled=True)]
    broadcast_in_dim x6 -> x0, local copies, waits for them, and re-layouts: 11.4 us -> none  [per_device(): combined = jnp.where(chosen, kernel[tap_index], combined)]
    select_n x3 -> x0, local copies, waits for them, and re-layouts: 10.7 us -> none  [per_device(): combined = jnp.where(chosen, kernel[tap_index], combined)]
    select_n x2 -> x0, other arithmetic: 6.87 us -> none  [per_device(): combined = jnp.where(chosen, kernel[tap_index], combined)]
    unnamed x53 -> x1, local copies, waits for them, and re-layouts: 6.97 us -> 2.94 us
  transfers between devices with their start and end apart: 5 -> 0, of which waited for: 5 -> 0; matrix products, arithmetic and copies ran while one was open for 8% -> 0% of each run, Pallas kernels for 0% -> 0%
where the time goes in v1:
time: 53.2 us; the launch traced here: 53.1 us
  Pallas kernels  50.1 us (94%)
  local copies, waits for them, and re-layouts  2.94 us (6%)
    pallas_call x1, Pallas kernels, per_device(): pl.pallas_call(functools.partial(kernel, n_obs, n_src), out_shape=jax.Sha...  50.1 us
    unnamed x1, local copies, waits for them, and re-layouts  2.94 us

profile of v1, /device:TPU:0, one launch (start us, length us, event | category | flops | bytes accessed | tf_op | source)
XLA Modules:
  0.0 53.1 jit_solution(6196497726120765682)
XLA Ops:
  0.0 50.1 %shard_map.73 = bf16[5,2,64,1536]{3,2,1,0:T(8,128)(2,1)} custom-call(bf16[3,2,64,1536]{3,2,1,0:T(8,128)(2,1)} %hist_ref.1, bf16[5,2,64,1536]{3,2,1,0:T(8,128)(2,1)} %inc_ref.1, bf16[2,64,1536]{2,1,0:T(8,128)(2,1)} %proj_ref.1, bf16[2,64,1536]{2,1,0:T(8,128)(2,1)} %expand_ref.1, bf16[2,1536,1536]{2,1,0:T(8,128)(2,1)} %near_ref.1, ...), custom_call_target="tpu_custom_call" | custom-call | tf_op jit(solution)/shard_map/pallas_call | solution.py:244
  50.1 2.9 %copy.12 = bf16[5,2,64,1536]{3,2,1,0:T(8,128)(2,1)} copy(bf16[5,2,64,1536]{3,2,1,0:T(8,128)(2,1)} %shard_map.73) | data formatting | bytes 3932160

commit v2 on v1

--- a/solution.py
+++ b/solution.py
@@ -41,6 +41,14 @@
     sources = lag_ref.shape[2]
     tile = 256
 
+    barrier = pltpu.get_barrier_semaphore()
+    src_peers = [partner(s, turn, n_src) for turn in range(1, n_src)]
+    obs_peers = [partner(o, turn, n_obs) for turn in range(1, n_obs)]
+    for peer in src_peers:
+        pl.semaphore_signal(barrier, inc=1, device_id=(o, peer), device_id_type=MESH)
+    for peer in obs_peers:
+        pl.semaphore_signal(barrier, inc=1, device_id=(peer, s), device_id_type=MESH)
+
     loads = []
 
     def load(src, dst):
@@ -62,14 +70,6 @@
         mine.append(load(near_ref.at[c], nv.at[c]))
         n_loads.append(mine)
 
-    barrier = pltpu.get_barrier_semaphore()
-    src_peers = [partner(s, turn, n_src) for turn in range(1, n_src)]
-    obs_peers = [partner(o, turn, n_obs) for turn in range(1, n_obs)]
-    for peer in src_peers:
-        pl.semaphore_signal(barrier, inc=1, device_id=(o, peer), device_id_type=MESH)
-    for peer in obs_peers:
-        pl.semaphore_signal(barrier, inc=1, device_id=(peer, s), device_id_type=MESH)
-
     for c in range(clusters):
         for k in range(clusters):
             if k != c:
@@ -99,7 +99,12 @@
             src_ref=sendp.at[step, at], dst_ref=recvp.at[step, slot], send_sem=ps_sem.at[step, turn],
             recv_sem=pr_sem.at[step, slot], device_id=(obs_peers[turn], s), device_id_type=MESH)
 
-    for turn in range(n_src - 1):
+    group = 2 if n_src % 2 == 0 else 1
+    relayed = group == 2 and n_src & (n_src - 1) == 0
+    beside = n_src - 2
+    direct = [turn for turn in range(n_src - 1) if not relayed or turn == beside or (n_src - 1 - turn) % 2 == 0]
+    far = [turn for turn in direct if turn != beside] if relayed else []
+    for turn in direct:
         h_copy(turn, s).start()
 
     for copy in c_loads:
@@ -147,13 +152,39 @@
             bv[...] += value[:steps * excite]
         mv[c * rank:(c + 1) * rank] = value[steps * excite:].astype(BF16)
 
-    keep(0, near(0))
-
+    def forward(turn):
+        return pltpu.make_async_remote_copy(
+            src_ref=qh.at[src_peers[turn]], dst_ref=qh.at[src_peers[turn]], send_sem=hs_sem.at[turn - 1],
+            recv_sem=hr_sem.at[src_peers[turn]], device_id=(o, src_peers[beside]), device_id_type=MESH)
+
+    for turn in reversed(far):
+        h_copy(turn, src_peers[turn]).wait_recv()
+        forward(turn).start()
     for turn in range(n_src - 1):
-        h_copy(turn, src_peers[turn]).wait_recv()
+        if turn not in far:
+            h_copy(turn, src_peers[turn]).wait_recv()
+
+    pairs = n_src // group
+    own_pair = s // group
+    ordered = [own_pair] + [partner(own_pair, turn, pairs) for turn in range(pairs - 1, 0, -1)]
 
     def gathered(ref):
         return jnp.concatenate([ref[k] for k in range(n_src)], axis=1)
+
+    def newest_term(step, total):
+        for place, pair in enumerate(ordered):
+            for k in range(group):
+                if place > 0:
+                    q_copy(step, 0, pair * group + k).wait_recv()
+                elif group == 2 and k == 0:
+                    q_copy(step, 0, partner_slot).wait_recv()
+            part = jnp.concatenate([qn[step, pair * group + k] for k in range(group)], axis=1)
+            deep = group * width
+            rows_at = pl.ds(pl.multiple_of(pair * deep, deep), deep)
+            total = total + jnp.dot(part, wv[0, rows_at, :], preferred_element_type=F32)
+        return total
+
+    partner_slot = own_pair * 2 + (1 - s % 2)
 
     def slot_of(ref, k):
         return jnp.concatenate([ref[j, k * excite:(k + 1) * excite] for j in range(n_src)], axis=1)
@@ -180,7 +211,7 @@
     for ahead in range(hist, steps):
         base[ahead] = jnp.zeros((excite, n_obs * width), F32)
 
-    for c in range(1, clusters):
+    for c in range(clusters):
         keep(c, near(c))
 
     outs = []
@@ -207,18 +238,18 @@
         for turn in range(n_src - 1):
             q_copy(step, turn, s).start()
         finish(step, field)
-        for turn in range(n_src - 1):
-            q_copy(step, turn, src_peers[turn]).wait_recv()
+        send_partial(step + 1, newest_term(step, base[step + 1]))
         columns = gathered(qn.at[step])
-        send_partial(step + 1, base[step + 1] + jnp.dot(columns, wv[0], preferred_element_type=F32))
         for d in range(2, hist + 1):
             if step + d < steps:
                 base[step + d] += jnp.dot(columns, wv[d - 1], preferred_element_type=F32)
 
     for copy in outs:
         copy.wait()
-    for turn in range(n_src - 1):
+    for turn in direct:
         h_copy(turn, s).wait_send()
+    for turn in far:
+        forward(turn).wait_send()
     for step in range(steps):
         for turn in range(n_obs - 1):
             p_copy(step, turn, obs_peers[turn], o).wait_send()

time: 53.2 us -> 55.1 us (1.036)
  Pallas kernels: 50.1 us -> 52 us
    pallas_call x1, Pallas kernels: 50.1 us -> 52 us  [per_device(): pl.pallas_call(functools.partial(kernel, n_obs, n_src), out_shape=jax.Sha...]
where the time goes in v2:
time: 55.1 us; the launch traced here: 55 us
  Pallas kernels  52 us (94%)
  local copies, waits for them, and re-layouts  2.94 us (5%)
    pallas_call x1, Pallas kernels, per_device(): pl.pallas_call(functools.partial(kernel, n_obs, n_src), out_shape=jax.Sha...  52 us
    unnamed x1, local copies, waits for them, and re-layouts  2.94 us

profile of v2, /device:TPU:0, one launch (start us, length us, event | category | flops | bytes accessed | tf_op | source)
XLA Modules:
  0.0 55.0 jit_solution(11279055541777580592)
XLA Ops:
  0.0 52.0 %shard_map.73 = bf16[5,2,64,1536]{3,2,1,0:T(8,128)(2,1)} custom-call(bf16[3,2,64,1536]{3,2,1,0:T(8,128)(2,1)} %hist_ref.1, bf16[5,2,64,1536]{3,2,1,0:T(8,128)(2,1)} %inc_ref.1, bf16[2,64,1536]{2,1,0:T(8,128)(2,1)} %proj_ref.1, bf16[2,64,1536]{2,1,0:T(8,128)(2,1)} %expand_ref.1, bf16[2,1536,1536]{2,1,0:T(8,128)(2,1)} %near_ref.1, ...), custom_call_target="tpu_custom_call" | custom-call | tf_op jit(solution)/shard_map/pallas_call | solution.py:275
  52.0 2.9 %copy.12 = bf16[5,2,64,1536]{3,2,1,0:T(8,128)(2,1)} copy(bf16[5,2,64,1536]{3,2,1,0:T(8,128)(2,1)} %shard_map.73) | data formatting | bytes 3932160

commit v3 on v2

--- a/solution.py
+++ b/solution.py
@@ -100,11 +100,7 @@
             recv_sem=pr_sem.at[step, slot], device_id=(obs_peers[turn], s), device_id_type=MESH)
 
     group = 2 if n_src % 2 == 0 else 1
-    relayed = group == 2 and n_src & (n_src - 1) == 0
-    beside = n_src - 2
-    direct = [turn for turn in range(n_src - 1) if not relayed or turn == beside or (n_src - 1 - turn) % 2 == 0]
-    far = [turn for turn in direct if turn != beside] if relayed else []
-    for turn in direct:
+    for turn in range(n_src - 1):
         h_copy(turn, s).start()
 
     for copy in c_loads:
@@ -152,17 +148,10 @@
             bv[...] += value[:steps * excite]
         mv[c * rank:(c + 1) * rank] = value[steps * excite:].astype(BF16)
 
-    def forward(turn):
-        return pltpu.make_async_remote_copy(
-            src_ref=qh.at[src_peers[turn]], dst_ref=qh.at[src_peers[turn]], send_sem=hs_sem.at[turn - 1],
-            recv_sem=hr_sem.at[src_peers[turn]], device_id=(o, src_peers[beside]), device_id_type=MESH)
-
-    for turn in reversed(far):
+    keep(0, near(0))
+
+    for turn in range(n_src - 1):
         h_copy(turn, src_peers[turn]).wait_recv()
-        forward(turn).start()
-    for turn in range(n_src - 1):
-        if turn not in far:
-            h_copy(turn, src_peers[turn]).wait_recv()
 
     pairs = n_src // group
     own_pair = s // group
@@ -211,7 +200,7 @@
     for ahead in range(hist, steps):
         base[ahead] = jnp.zeros((excite, n_obs * width), F32)
 
-    for c in range(clusters):
+    for c in range(1, clusters):
         keep(c, near(c))
 
     outs = []
@@ -246,16 +235,28 @@
 
     for copy in outs:
         copy.wait()
-    for turn in direct:
+    for turn in range(n_src - 1):
         h_copy(turn, s).wait_send()
-    for turn in far:
-        forward(turn).wait_send()
     for step in range(steps):
         for turn in range(n_obs - 1):
             p_copy(step, turn, obs_peers[turn], o).wait_send()
         if step + 1 < steps:
             for turn in range(n_src - 1):
                 q_copy(step, turn, s).wait_send()
+
+
+def hand_on(made_ref, out_ref, held, in_sem, out_sem):
+    steps, clusters = made_ref.shape[:2]
+    places = [(t, c) for t in range(steps) for c in range(clusters)]
+    taken = [pltpu.make_async_copy(made_ref.at[t, c], held.at[t, c], in_sem.at[t, c]) for t, c in places]
+    given = [pltpu.make_async_copy(held.at[t, c], out_ref.at[t, c], out_sem.at[t, c]) for t, c in places]
+    for copy in taken:
+        copy.start()
+    for before, after in zip(taken, given):
+        before.wait()
+        after.start()
+    for copy in given:
+        copy.wait()
 
 
 def per_device(n_obs, n_src, history, incident, proj_basis, expand_basis, near_inverse, couplings, lags):
@@ -272,7 +273,7 @@
     loads = clusters * (1 + hist + steps + 2) + 1
     any_spec = pl.BlockSpec(memory_space=pl.ANY)
     dma = pltpu.SemaphoreType.DMA
-    return pl.pallas_call(
+    made = pl.pallas_call(
         functools.partial(kernel, n_obs, n_src),
         out_shape=jax.ShapeDtypeStruct(incident.shape, BF16),
         in_specs=[any_spec] * 6 + [pl.BlockSpec(memory_space=pltpu.SMEM)],
@@ -308,6 +309,14 @@
             collective_id=0, has_side_effects=True, vmem_limit_bytes=63000 * 1024
         ),
     )(history, incident, proj_basis, expand_basis, near_inverse, flat, lag_table)
+    return pl.pallas_call(
+        hand_on,
+        out_shape=jax.ShapeDtypeStruct(incident.shape, BF16),
+        in_specs=[any_spec],
+        out_specs=any_spec,
+        scratch_shapes=[pltpu.VMEM(incident.shape, BF16), dma((steps, clusters)), dma((steps, clusters))],
+        compiler_params=pltpu.CompilerParams(vmem_limit_bytes=63000 * 1024),
+    )(made)
 
 
 def solution(mesh):

time: 55.1 us -> 52.3 us (0.949)
  local copies, waits for them, and re-layouts: 2.94 us -> 0 us
    unnamed x1 -> x0, local copies, waits for them, and re-layouts: 2.94 us -> none
    pallas_call x0 -> x1, Pallas kernels: none -> 2.46 us  [per_device(): pl.pallas_call(hand_on, out_shape=jax.ShapeDtypeStruct(incident.shape, BF...]
    pallas_call x1, Pallas kernels: 52 us -> 49.7 us  [per_device(): pl.pallas_call(functools.partial(kernel, n_obs, n_src), out_shape=jax.Sha...]
where the time goes in v3:
time: 52.3 us; the launch traced here: 52.2 us
  Pallas kernels  52.1 us (100%)
    pallas_call x1, Pallas kernels, per_device(): pl.pallas_call(functools.partial(kernel, n_obs, n_src), out_shape=jax.Sha...  49.7 us
    pallas_call x1, Pallas kernels, per_device(): pl.pallas_call(hand_on, out_shape=jax.ShapeDtypeStruct(incident.shape, BF...  2.46 us

profile of v3, /device:TPU:0, one launch (start us, length us, event | category | flops | bytes accessed | tf_op | source)
XLA Modules:
  0.0 52.2 jit_solution(6853794154288572814)
XLA Ops:
  0.0 49.7 %shard_map.73.made_ref = bf16[5,2,64,1536]{3,2,1,0:T(8,128)(2,1)} custom-call(bf16[3,2,64,1536]{3,2,1,0:T(8,128)(2,1)} %hist_ref.1, bf16[5,2,64,1536]{3,2,1,0:T(8,128)(2,1)} %inc_ref.1, bf16[2,64,1536]{2,1,0:T(8,128)(2,1)} %proj_ref.1, bf16[2,64,1536]{2,1,0:T(8,128)(2,1)} %expand_ref.1, bf16[2,1536,1536]{2,1,0:T(8,128)(2,1)} %near_ref.1, ...), custom_call_target="tpu_custom_call" | custom-call | tf_op jit(solution)/shard_map/pallas_call | solution.py:276
  49.7 2.5 %shard_map.74 = bf16[5,2,64,1536]{3,2,1,0:T(8,128)(2,1)} custom-call(bf16[5,2,64,1536]{3,2,1,0:T(8,128)(2,1)} %shard_map.73.made_ref), custom_call_target="tpu_custom_call" | custom-call | tf_op jit(solution)/shard_map/pallas_call | solution.py:312
